TPU v7x, 32 devices: a whole 2x2x4 slice. The times are simulated.
32 devices in a mesh: seg: 8 (over y, x, core), head: 4 (over z).
Axes of the slice: x: 2, y: 2, z: 4, core: 2. Of those that a mesh axis runs over, the one named last changes fastest.
Arguments:
- layer_input: bfloat16 [1, 4096, 2048], P(None, 'seg', 'head'), may hold values from -160 to 160, as said below
- w_qkv: bfloat16 [2048, 3, 1024], P(None, None, 'head'), may hold values from -3 to 3
- comp_weight: bfloat16 [3, 2, 1024], P(None, None, 'head'), may hold values from -2.5 to 2.5
- w_out: bfloat16 [1024, 2048], P('seg', 'head'), may hold values from -1.5 to 1.5
Outputs:
- attn_out: bfloat16 [1, 4096, 2048], P(None, 'seg', 'head')
Inputs may be any that keep to these rules, and one draw needn't show every extreme that they name: layer_input varies in scale from feature to feature and from token to token.
All inputs are finite; a program needn't handle non-finite values.
Results may differ from a plain program's by a relative error of at most 0.0089.
Values may be sent and summed in bfloat16 or wider, within the bound.
No kernel may reach another device: no remote copies, remote signals or barrier semaphores. Data moves between devices by JAX's collectives and lax.ppermute only.
A program may use at most 64 MiB of HBM per device.

v0:
```python
import math
import jax
import jax.numpy as jnp
from jax import lax
from jax.sharding import PartitionSpec as P

DH = 128


def passed_along(block, axis, distance):
    devices = range(lax.axis_size(axis))
    route = [(i - distance, i) for i in devices if i - distance in devices]
    return lax.ppermute(block, axis, route)


def layer_norm(values):
    center_mean = jnp.mean(values, axis=-1, keepdims=True)
    centered = values - center_mean
    variance = jnp.mean(centered * centered, axis=-1, keepdims=True)
    return centered * lax.rsqrt(variance + 1e-05)


def compress_block(source, weight):
    batch, pair, length, width = source.shape
    grouped = source.reshape(batch, pair, length // 3, 3, width)
    mixed = jnp.einsum("bkltc,tkc->bklc", grouped, weight, preferred_element_type=jnp.float32)
    return mixed.astype(jnp.bfloat16)


def key_allowed(seg_len, segment):
    query_pos = jnp.arange(seg_len)[:, None]
    key_pos = jnp.arange(3 * seg_len)[None, :]
    own_part = (key_pos >= 2 * seg_len) & (key_pos - 2 * seg_len <= query_pos)
    memory_part = (key_pos >= seg_len) & (key_pos < 2 * seg_len) & (segment >= 1)
    comp_part = (key_pos < seg_len) & (segment >= 4)
    return own_part | memory_part | comp_part


def attend(queries, key_vals, segment):
    batch, seg_len, width = queries.shape
    heads_here = width // DH
    query_heads = queries.reshape(batch, seg_len, heads_here, DH)
    key_heads = key_vals[:, 0].reshape(batch, 3 * seg_len, heads_here, DH)
    value_heads = key_vals[:, 1].reshape(batch, 3 * seg_len, heads_here, DH)
    scores = jnp.einsum(
        "bqhd,bkhd->bhqk", query_heads, key_heads, preferred_element_type=jnp.float32
    )
    scores = scores / math.sqrt(DH)
    allowed = key_allowed(seg_len, segment)
    scores = jnp.where(allowed[None, None], scores, jnp.float32(-1e30))
    highest = jnp.max(scores, axis=-1, keepdims=True)
    exponent = jnp.exp(scores - highest)
    weights = (exponent / jnp.sum(exponent, axis=-1, keepdims=True)).astype(jnp.bfloat16)
    mixed = jnp.einsum("bhqk,bkhd->bqhd", weights, value_heads, preferred_element_type=jnp.float32)
    return mixed.astype(jnp.bfloat16).reshape(batch, seg_len, width)


def local(layer_input, w_qkv, comp_weight, w_out):
    gathered = lax.all_gather(layer_input, "head", axis=2, tiled=True)
    normed = layer_norm(gathered.astype(jnp.float32)).astype(jnp.bfloat16)
    projected = jnp.einsum("bld,dkc->bklc", normed, w_qkv, preferred_element_type=jnp.float32)
    projected = projected.astype(jnp.bfloat16)
    queries = projected[:, 0]
    key_vals = projected[:, 1:3]
    memory = passed_along(key_vals, "seg", 1)
    second_back = passed_along(memory, "seg", 1)
    upcoming = compress_block(jnp.concatenate([second_back, memory, key_vals], axis=2), comp_weight)
    compressed = passed_along(upcoming, "seg", 2)
    segment = lax.axis_index("seg")
    joined = jnp.concatenate([compressed, memory, key_vals], axis=2)
    context = attend(queries, joined, segment)
    full_ctx = lax.all_gather(context, "head", axis=2, tiled=True)
    whole_out = lax.all_gather(w_out, "seg", axis=0, tiled=True)
    result_sum = jnp.einsum("blr,rc->blc", full_ctx, whole_out, preferred_element_type=jnp.float32)
    return result_sum.astype(jnp.bfloat16)


def solution(mesh):
    return jax.shard_map(
        local,
        mesh=mesh,
        in_specs=(
            P(None, "seg", "head"),
            P(None, None, "head"),
            P(None, None, "head"),
            P("seg", "head"),
        ),
        out_specs=P(None, "seg", "head"),
        check_vma=False,
    )
```

profile of v0, /device:TPU:0, one launch (start us, length us, event | category | flops | bytes accessed | tf_op | source)
XLA Modules:
  0.0 164.3 jit_solution(6512609901003673193)
XLA Ops:
  7.4 0.7 all-gather.4.cloned.1.call-update
  8.1 0.0 all-gather.8.cloned.1.call-start
  8.1 50.0 %all-gather.4.cloned.1.call-done = bf16[1,512,2048]{2,1,0:T(8,128)(2,1)} async-done(((bf16[1,512,512]{2,1,0:T(8,128)(2,1)}), bf16[1,512,2048]{2,1,0:T(8,128)(2,1)}) %all-gather.4.cloned.1.call-update) | async-done | bytes 2097168 | tf_op jit(solution)/shard_map/all_gather | solution.py:59
  58.2 2.1 %convert_reduce_fusion = f32[512]{0:T(512)S(1)} fusion(bf16[1,512,2048]{2,1,0:T(8,128)(2,1)} %all-gather.4.cloned.1.call-done), kind=kLoop, calls=%fused_computation.6 | loop fusion | flops 2096640 | bytes 2099200 | tf_op jit(solution)/shard_map/reduce_sum | solution.py:17
  60.3 0.1 copy-done.1
  60.4 0.7 fusion.4
  61.1 0.0 copy-start.4
  61.1 2.0 %fusion.21 = bf16[1,3,512,256]{2,3,1,0:T(8,128)(2,1)S(1)} fusion(bf16[2048,3,256]{2,0,1:T(8,128)(2,1)S(1)} %copy-done, bf16[1,512,2048]{2,1,0:T(8,128)(2,1)S(1)} %copy-done.1, f32[512]{0:T(512)S(1)} %add_rsqrt_fusion, f32[512]{0:T(512)S(1)} %broadcast_multiply_fusion), kind=kOutput, calls=%fused_computation.29 | convolution fusion | flops 1615200256 | bytes 6033408 | tf_op jit(solution)/shard_map/bld,dkc->bklc/dot_general | solution.py:61
  63.1 0.0 copy-start.2
  63.1 0.8 copy-done.2
  64.0 2.4 %collective-permute-start = (bf16[1,2,512,256]{2,3,1,0:T(8,128)(2,1)S(1)}, bf16[1,2,512,256]{2,3,1,0:T(8,128)(2,1)}, u32[]{:S(2)}, u32[]{:S(2)}) collective-permute-start(bf16[1,2,512,256]{2,3,1,0:T(8,128)(2,1)S(1)} %slice.16), channel_id=1, source_target_pairs={{0,4},{4,8},{8,12},{12,16},{16,20},{20,24},{24,28},{1,5},{5,9},{9,... | collective-permute-start | bytes 1572872 | tf_op jit(solution)/shard_map/ppermute | solution.py:13
  66.4 0.8 collective-permute-done
  67.2 9.1 %collective-permute-start.1 = (bf16[1,2,512,256]{2,3,1,0:T(8,128)(2,1)}, bf16[1,2,512,256]{2,3,1,0:T(8,128)(2,1)}, u32[]{:S(2)}, u32[]{:S(2)}) collective-permute-start(bf16[1,2,512,256]{2,3,1,0:T(8,128)(2,1)} %collective-permute-done), channel_id=1, source_target_pairs={{0,4},{4,8},{8,12},{12,16},{16,20},{20,24},{24,28},{1,5},{5,9},{9,... | collective-permute-start | bytes 1572872 | tf_op jit(solution)/shard_map/ppermute | solution.py:13
  76.3 0.0 all-gather.8.cloned.1.call-update
  76.3 0.0 all-gather.6.cloned.1.call-start
  76.4 0.9 collective-permute-done.1
  77.3 2.6 %pad_maximum_fusion.1 = bf16[1,2,1536,256]{2,3,1,0:T(8,128)(2,1)} fusion(bf16[1,2,512,256]{2,3,1,0:T(8,128)(2,1)} %copy-done.2, bf16[1,2,512,256]{2,3,1,0:T(8,128)(2,1)} %collective-permute-done, bf16[1,2,512,256]{2,3,1,0:T(8,128)(2,1)} %collective-permute-done.1), kind=kLoop, calls=%fused_computation.25 | loop fusion | flops 4718592 | bytes 3145728 | tf_op jit(solution)/shard_map/concatenate | solution.py:67
  80.0 4.9 %copy.23 = bf16[1,2,1536,256]{3,1,2,0:T(2,128)(2,1)} copy(bf16[1,2,1536,256]{2,3,1,0:T(8,128)(2,1)} %pad_maximum_fusion.1) | data formatting | bytes 3145728
  84.9 5.0 %multiply_reduce_fusion = bf16[2,256,512]{1,0,2:T(2,128)(2,1)} fusion(bf16[2,256,3,512]{1,0,2,3:T(2,128)(2,1)} %bitcast.45, f32[2,256,3]{1,0,2:T(2,128)S(1)} %bitcast_convert_fusion), kind=kLoop, calls=%fused_computation.11 | loop fusion | flops 2097152 | bytes 2103296
  89.9 2.0 %copy.20 = bf16[2,256,512]{2,1,0:T(8,128)(2,1)} copy(bf16[2,256,512]{1,0,2:T(2,128)(2,1)} %multiply_reduce_fusion) | data formatting | bytes 1048576 | tf_op jit(solution)/shard_map/bkltc,tkc->bklc/dot_general | solution.py:26
  91.9 11.8 %collective-permute-start.2 = (bf16[1,2,512,256]{2,3,1,0:T(8,128)(2,1)}, bf16[1,2,512,256]{2,3,1,0:T(8,128)(2,1)S(1)}, u32[]{:S(2)}, u32[]{:S(2)}) collective-permute-start(bf16[1,2,512,256]{2,3,1,0:T(8,128)(2,1)} %bitcast.49), channel_id=1, source_target_pairs={{0,8},{4,12},{8,16},{12,20},{16,24},{20,28},{1,9},{5,13},{9,17},{1... | collective-permute-start | bytes 1572872 | tf_op jit(solution)/shard_map/ppermute | solution.py:13
  103.7 1.6 fusion.10
  105.3 1.0 slice.18
  106.3 9.7 %collective-permute-done.2 = bf16[1,2,512,256]{2,3,1,0:T(8,128)(2,1)S(1)} collective-permute-done((bf16[1,2,512,256]{2,3,1,0:T(8,128)(2,1)}, bf16[1,2,512,256]{2,3,1,0:T(8,128)(2,1)S(1)}, u32[]{:S(2)}, u32[]{:S(2)}) %collective-permute-start.2) | collective-permute-done | bytes 524320 | tf_op jit(solution)/shard_map/ppermute | solution.py:13
  116.0 1.3 pad_maximum_fusion
  117.3 1.3 fusion.39
  118.6 3.8 %fusion.40 = f32[2,512]{1,0:T(2,128)S(1)} fusion(pred[512,1536]{1,0:T(8,128)(4,1)} %fusion.10, bf16[512,2,128]{0,2,1:T(8,128)(2,1)S(1)} %bitcast.50, bf16[1536,2,128]{0,2,1:T(8,128)(2,1)} %bitcast.46), kind=kOutput, calls=%fused_computation.53 | convolution fusion | flops 408946176 | bytes 1839104 | tf_op jit(solution)/shard_map/sub | solution.py:52
  122.5 5.2 %fusion.25 = bf16[2,128,512]{2,1,0:T(8,128)(2,1)} fusion(bf16[1536,2,128]{0,2,1:T(8,128)(2,1)} %bitcast.48, f32[2,512]{1,0:T(2,128)S(1)} %fusion.40, pred[512,1536]{1,0:T(8,128)(4,1)} %fusion.10, bf16[512,2,128]{0,2,1:T(8,128)(2,1)S(1)} %bitcast.51, bf16[1536,2,128]{0,2,1:T(8,128)(2,1)} %bitcast.47), kind=kOutput, calls=%fused_computation.32 | convolution fusion | flops 813304320 | bytes 2887680 | tf_op jit(solution)/shard_map/bhqk,bkhd->bqhd/dot_general | solution.py:54
  127.6 0.0 all-gather.6.cloned.1.call-update
  127.7 0.0 all-gather.8.cloned.1.call-done
  127.7 26.1 %all-gather.6.cloned.1.call-done = bf16[1,512,1024]{1,2,0:T(8,128)(2,1)} async-done(((bf16[1,512,256]{1,2,0:T(8,128)(2,1)}), bf16[1,512,1024]{1,2,0:T(8,128)(2,1)}) %all-gather.6.cloned.1.call-update) | async-done | bytes 1048592 | tf_op jit(solution)/shard_map/all_gather | solution.py:72
  153.8 3.1 %fusion.24 = bf16[1,512,512]{2,1,0:T(8,128)(2,1)} fusion(bf16[1024,512]{1,0:T(8,128)(2,1)} %all-gather.8.cloned.1.call-done, bf16[1,512,1024]{1,2,0:T(8,128)(2,1)} %all-gather.6.cloned.1.call-done), kind=kOutput, calls=%fused_computation.31 | convolution fusion | flops 537133056 | bytes 2621440 | tf_op jit(solution)/shard_map/blr,rc->blc/dot_general | solution.py:74
  (14 shorter events, 0.1 us)
Async XLA Ops:
  7.4 53.7 %copy-start = (bf16[2048,3,256]{2,0,1:T(8,128)(2,1)S(1)}, bf16[2048,3,256]{2,0,1:T(8,128)(2,1)}, u32[]{:S(2)}) copy-start(bf16[2048,3,256]{2,0,1:T(8,128)(2,1)} %param.5) | copy-start | bytes 9437188
  7.4 50.8 %all-gather.4.cloned.1.call-start = ((), (), s32[]{:S(2)}) async-start(), calls=%async_computation | async-start | bytes 2621440 | tf_op jit(solution)/shard_map/all_gather | solution.py:59
  8.1 119.6 %all-gather.8.cloned.1.call-start = ((), (), s32[]{:S(2)}) async-start(), calls=%async_computation.2 | async-start | bytes 1179648 | tf_op jit(solution)/shard_map/all_gather | solution.py:73
  58.1 2.2 %copy-start.1 = (bf16[1,512,2048]{2,1,0:T(8,128)(2,1)S(1)}, bf16[1,512,2048]{2,1,0:T(8,128)(2,1)}, u32[]{:S(2)}) copy-start(bf16[1,512,2048]{2,1,0:T(8,128)(2,1)} %all-gather.4.cloned.1.call-done) | copy-start | bytes 6291460
  61.1 15.3 %copy-start.4 = (bf16[3,2,256]{2,1,0:T(2,128)(2,1)S(1)}, bf16[3,2,256]{2,1,0:T(2,128)(2,1)}, u32[]{:S(2)}) copy-start(bf16[3,2,256]{2,1,0:T(2,128)(2,1)} %param.6) | copy-start | bytes 9220
  63.1 4.1 %copy-start.3 = (bf16[1,3,512,256]{2,3,1,0:T(8,128)(2,1)}, bf16[1,3,512,256]{2,3,1,0:T(8,128)(2,1)S(1)}, u32[]{:S(2)}) copy-start(bf16[1,3,512,256]{2,3,1,0:T(8,128)(2,1)S(1)} %fusion.21) | copy-start | bytes 2359300
  63.1 0.9 copy-start.2
  64.0 3.2 %collective-permute-start = (bf16[1,2,512,256]{2,3,1,0:T(8,128)(2,1)S(1)}, bf16[1,2,512,256]{2,3,1,0:T(8,128)(2,1)}, u32[]{:S(2)}, u32[]{:S(2)}) collective-permute-start(bf16[1,2,512,256]{2,3,1,0:T(8,128)(2,1)S(1)} %slice.16), channel_id=1, source_target_pairs={{0,4},{4,8},{8,12},{12,16},{16,20},{20,24},{24,28},{1,5},{5,9},{9,... | collective-permute-start | bytes 1572872 | tf_op jit(solution)/shard_map/ppermute | solution.py:13
  67.2 10.1 %collective-permute-start.1 = (bf16[1,2,512,256]{2,3,1,0:T(8,128)(2,1)}, bf16[1,2,512,256]{2,3,1,0:T(8,128)(2,1)}, u32[]{:S(2)}, u32[]{:S(2)}) collective-permute-start(bf16[1,2,512,256]{2,3,1,0:T(8,128)(2,1)} %collective-permute-done), channel_id=1, source_target_pairs={{0,4},{4,8},{8,12},{12,16},{16,20},{20,24},{24,28},{1,5},{5,9},{9,... | collective-permute-start | bytes 1572872 | tf_op jit(solution)/shard_map/ppermute | solution.py:13
  76.3 77.5 %all-gather.6.cloned.1.call-start = ((), (), s32[]{:S(2)}) async-start(), calls=%async_computation.1 | async-start | bytes 1310720 | tf_op jit(solution)/shard_map/all_gather | solution.py:72
  91.9 24.1 %collective-permute-start.2 = (bf16[1,2,512,256]{2,3,1,0:T(8,128)(2,1)}, bf16[1,2,512,256]{2,3,1,0:T(8,128)(2,1)S(1)}, u32[]{:S(2)}, u32[]{:S(2)}) collective-permute-start(bf16[1,2,512,256]{2,3,1,0:T(8,128)(2,1)} %bitcast.49), channel_id=1, source_target_pairs={{0,8},{4,12},{8,16},{12,20},{16,24},{20,28},{1,9},{5,13},{9,17},{1... | collective-permute-start | bytes 1572872 | tf_op jit(solution)/shard_map/ppermute | solution.py:13
Sparse Core Ops, SparseCore 0:
  9.7 48.3 all-gather.3
Sparse Core Ops, SparseCore 1:
  76.4 23.4 all-gather.7
  127.7 26.0 all-gather.5
where the time goes:
time: 165 us; the launch traced here: 164 us
  waiting for transfers between devices  88.4 us (54%)
  starting transfers between devices  23.3 us (14%)
  between operations  15 us (9%)
  matrix products  14.1 us (9%)
  other arithmetic  13.4 us (8%)
  local copies, waits for them, and re-layouts  10.2 us (6%)
    all_gather x1, waiting for transfers between devices, local(): gathered = lax.all_gather(layer_input, 'head', axis=2, tiled=True)  50 us
    all_gather x1, waiting for transfers between devices, local(): full_ctx = lax.all_gather(context, 'head', axis=2, tiled=True)  26.1 us
    ppermute x3, starting transfers between devices, passed_along(): return lax.ppermute(block, axis, route)  23.2 us
    ppermute x3, waiting for transfers between devices, passed_along(): return lax.ppermute(block, axis, route)  11.5 us
    unnamed x11, local copies, waits for them, and re-layouts  5.9 us
    dot_general x1, matrix products, attend(): jnp.einsum('bhqk,bkhd->bqhd', weights, value_heads, preferred_element_typ...  5.18 us
    unnamed x2, other arithmetic  5.02 us
    sub x1, matrix products, attend(): exponent = jnp.exp(scores - highest)  3.83 us
  transfers between devices with their start and end apart: 6, of which 5 were waited for; matrix products, arithmetic and copies ran while one was open for 18% of the time, Pallas kernels for 0%

commit v1 on v0

--- a/solution.py
+++ b/solution.py
@@ -69,7 +69,7 @@
     segment = lax.axis_index("seg")
     joined = jnp.concatenate([compressed, memory, key_vals], axis=2)
     context = attend(queries, joined, segment)
-    full_ctx = lax.all_gather(context, "head", axis=2, tiled=True)
+    full_ctx = jnp.concatenate(lax.all_gather(context, "head"), axis=2)
     whole_out = lax.all_gather(w_out, "seg", axis=0, tiled=True)
     result_sum = jnp.einsum("blr,rc->blc", full_ctx, whole_out, preferred_element_type=jnp.float32)
     return result_sum.astype(jnp.bfloat16)

time: 165 us -> 189 us (1.15)
  waiting for transfers between devices: 88.4 us -> 111 us
  local copies, waits for them, and re-layouts: 10.2 us -> 14.3 us
    all_gather x1, waiting for transfers between devices: 0.03 us -> 22.4 us  [local(): whole_out = lax.all_gather(w_out, 'seg', axis=0, tiled=True)]
    all_gather x0 -> x1, local copies, waits for them, and re-layouts: none -> 2.28 us  [local(): full_ctx = jnp.concatenate(lax.all_gather(context, 'head'), axis=2)]
  transfers between devices with their start and end apart: 6 -> 6, of which waited for: 5 -> 6; matrix products, arithmetic and copies ran while one was open for 18% -> 3% of each run, Pallas kernels for 0% -> 0%
where the time goes in v1:
time: 189 us
  waiting for transfers between devices  111 us (59%)
  starting transfers between devices  23.2 us (12%)
  local copies, waits for them, and re-layouts  14.3 us (8%)
  matrix products  14.1 us (7%)
  other arithmetic  13.4 us (7%)
  between operations  13.2 us (7%)
    all_gather x1, waiting for transfers between devices, local(): gathered = lax.all_gather(layer_input, 'head', axis=2, tiled=True)  50 us
    all_gather x1, waiting for transfers between devices, local(): full_ctx = jnp.concatenate(lax.all_gather(context, 'head'), axis=2)  26.2 us
    ppermute x3, starting transfers between devices, passed_along(): return lax.ppermute(block, axis, route)  23.1 us
    all_gather x1, waiting for transfers between devices, local(): whole_out = lax.all_gather(w_out, 'seg', axis=0, tiled=True)  22.4 us
    ppermute x3, waiting for transfers between devices, passed_along(): return lax.ppermute(block, axis, route)  10.7 us
    unnamed x11, local copies, waits for them, and re-layouts  5.9 us
    dot_general x1, matrix products, attend(): jnp.einsum('bhqk,bkhd->bqhd', weights, value_heads, preferred_element_typ...  5.18 us
    unnamed x2, other arithmetic  5.02 us
  transfers between devices with their start and end apart: 6, of which 6 were waited for; matrix products, arithmetic and copies ran while one was open for 3% of the time, Pallas kernels for 0%

profile of v1, /device:TPU:0, one launch (start us, length us, event | category | flops | bytes accessed | tf_op | source)
XLA Modules:
  0.0 188.8 jit_solution(2521154012238034137)
XLA Ops:
  6.5 0.7 all-gather.4.cloned.1.call-update
  7.3 0.0 all-gather.6.cloned.1.call-start
  7.3 50.0 %all-gather.4.cloned.1.call-done = bf16[1,512,2048]{2,1,0:T(8,128)(2,1)} async-done(((bf16[1,512,512]{2,1,0:T(8,128)(2,1)}), bf16[1,512,2048]{2,1,0:T(8,128)(2,1)}) %all-gather.4.cloned.1.call-update) | async-done | bytes 2097168 | tf_op jit(solution)/shard_map/all_gather | solution.py:59
  57.3 2.1 %convert_reduce_fusion = f32[512]{0:T(512)S(1)} fusion(bf16[1,512,2048]{2,1,0:T(8,128)(2,1)} %all-gather.4.cloned.1.call-done), kind=kLoop, calls=%fused_computation.6 | loop fusion | flops 2096640 | bytes 2099200 | tf_op jit(solution)/shard_map/reduce_sum | solution.py:17
  59.4 0.1 copy-done.1
  59.5 0.7 fusion.4
  60.3 2.0 %fusion.21 = bf16[1,3,512,256]{2,3,1,0:T(8,128)(2,1)S(1)} fusion(bf16[2048,3,256]{2,0,1:T(8,128)(2,1)S(1)} %copy-done, bf16[1,512,2048]{2,1,0:T(8,128)(2,1)S(1)} %copy-done.1, f32[512]{0:T(512)S(1)} %add_rsqrt_fusion, f32[512]{0:T(512)S(1)} %broadcast_multiply_fusion), kind=kOutput, calls=%fused_computation.29 | convolution fusion | flops 1615200256 | bytes 6033408 | tf_op jit(solution)/shard_map/bld,dkc->bklc/dot_general | solution.py:61
  62.3 0.8 copy-done.2
  63.2 2.4 %collective-permute-start = (bf16[1,2,512,256]{2,3,1,0:T(8,128)(2,1)S(1)}, bf16[1,2,512,256]{2,3,1,0:T(8,128)(2,1)}, u32[]{:S(2)}, u32[]{:S(2)}) collective-permute-start(bf16[1,2,512,256]{2,3,1,0:T(8,128)(2,1)S(1)} %slice.16), channel_id=1, source_target_pairs={{0,4},{4,8},{8,12},{12,16},{16,20},{20,24},{24,28},{1,5},{5,9},{9,... | collective-permute-start | bytes 1572872 | tf_op jit(solution)/shard_map/ppermute | solution.py:13
  65.5 0.8 collective-permute-done
  66.4 9.1 %collective-permute-start.1 = (bf16[1,2,512,256]{2,3,1,0:T(8,128)(2,1)}, bf16[1,2,512,256]{2,3,1,0:T(8,128)(2,1)}, u32[]{:S(2)}, u32[]{:S(2)}) collective-permute-start(bf16[1,2,512,256]{2,3,1,0:T(8,128)(2,1)} %collective-permute-done), channel_id=1, source_target_pairs={{0,4},{4,8},{8,12},{12,16},{16,20},{20,24},{24,28},{1,5},{5,9},{9,... | collective-permute-start | bytes 1572872 | tf_op jit(solution)/shard_map/ppermute | solution.py:13
  75.5 1.0 collective-permute-done.1
  76.5 2.6 %pad_maximum_fusion.1 = bf16[1,2,1536,256]{2,3,1,0:T(8,128)(2,1)} fusion(bf16[1,2,512,256]{2,3,1,0:T(8,128)(2,1)} %copy-done.2, bf16[1,2,512,256]{2,3,1,0:T(8,128)(2,1)} %collective-permute-done, bf16[1,2,512,256]{2,3,1,0:T(8,128)(2,1)} %collective-permute-done.1), kind=kLoop, calls=%fused_computation.25 | loop fusion | flops 4718592 | bytes 3145728 | tf_op jit(solution)/shard_map/concatenate | solution.py:67
  79.1 4.9 %copy.34 = bf16[1,2,1536,256]{3,1,2,0:T(2,128)(2,1)} copy(bf16[1,2,1536,256]{2,3,1,0:T(8,128)(2,1)} %pad_maximum_fusion.1) | data formatting | bytes 3145728
  84.0 5.0 %multiply_reduce_fusion = bf16[2,256,512]{1,0,2:T(2,128)(2,1)} fusion(bf16[2,256,3,512]{1,0,2,3:T(2,128)(2,1)} %bitcast.46, f32[2,256,3]{1,0,2:T(2,128)S(1)} %bitcast_convert_fusion), kind=kLoop, calls=%fused_computation.11 | loop fusion | flops 2097152 | bytes 2103296
  89.1 2.0 %copy.31 = bf16[2,256,512]{2,1,0:T(8,128)(2,1)} copy(bf16[2,256,512]{1,0,2:T(2,128)(2,1)} %multiply_reduce_fusion) | data formatting | bytes 1048576 | tf_op jit(solution)/shard_map/bkltc,tkc->bklc/dot_general | solution.py:26
  91.1 11.6 %collective-permute-start.2 = (bf16[1,2,512,256]{2,3,1,0:T(8,128)(2,1)}, bf16[1,2,512,256]{2,3,1,0:T(8,128)(2,1)S(1)}, u32[]{:S(2)}, u32[]{:S(2)}) collective-permute-start(bf16[1,2,512,256]{2,3,1,0:T(8,128)(2,1)} %bitcast.51), channel_id=1, source_target_pairs={{0,8},{4,12},{8,16},{12,20},{16,24},{20,28},{1,9},{5,13},{9,17},{1... | collective-permute-start | bytes 1572872 | tf_op jit(solution)/shard_map/ppermute | solution.py:13
  102.7 1.6 fusion.10
  104.4 1.0 slice.18
  105.3 8.8 %collective-permute-done.2 = bf16[1,2,512,256]{2,3,1,0:T(8,128)(2,1)S(1)} collective-permute-done((bf16[1,2,512,256]{2,3,1,0:T(8,128)(2,1)}, bf16[1,2,512,256]{2,3,1,0:T(8,128)(2,1)S(1)}, u32[]{:S(2)}, u32[]{:S(2)}) %collective-permute-start.2) | collective-permute-done | bytes 524320 | tf_op jit(solution)/shard_map/ppermute | solution.py:13
  114.1 1.3 pad_maximum_fusion
  115.4 1.3 fusion.38
  116.7 3.8 %fusion.39 = f32[2,512]{1,0:T(2,128)S(1)} fusion(pred[512,1536]{1,0:T(8,128)(4,1)} %fusion.10, bf16[512,2,128]{0,2,1:T(8,128)(2,1)S(1)} %bitcast.52, bf16[1536,2,128]{0,2,1:T(8,128)(2,1)} %bitcast.48), kind=kOutput, calls=%fused_computation.52 | convolution fusion | flops 408946176 | bytes 1839104 | tf_op jit(solution)/shard_map/sub | solution.py:52
  120.6 5.2 %fusion.25 = bf16[2,128,512]{2,1,0:T(8,128)(2,1)} fusion(bf16[1536,2,128]{0,2,1:T(8,128)(2,1)} %bitcast.50, f32[2,512]{1,0:T(2,128)S(1)} %fusion.39, pred[512,1536]{1,0:T(8,128)(4,1)} %fusion.10, bf16[512,2,128]{0,2,1:T(8,128)(2,1)S(1)} %bitcast.53, bf16[1536,2,128]{0,2,1:T(8,128)(2,1)} %bitcast.49), kind=kOutput, calls=%fused_computation.32 | convolution fusion | flops 813304320 | bytes 2887680 | tf_op jit(solution)/shard_map/bhqk,bkhd->bqhd/dot_general | solution.py:54
  125.7 1.8 copy.21
  127.6 0.0 all-gather.6.cloned.1.call-update
  127.6 0.0 all-gather.8.cloned.1.call-start
  127.6 0.7 all-gather.8.cloned.1.call-update
  128.3 26.2 %all-gather.6.cloned.1.call-done = bf16[4,1,512,256]{3,2,1,0:T(8,128)(2,1)} async-done(((bf16[1,1,512,256]{3,2,1,0:T(8,128)(2,1)}), bf16[4,1,512,256]{3,2,1,0:T(8,128)(2,1)}) %all-gather.6.cloned.1.call-update) | async-done | bytes 1048592 | tf_op jit(solution)/shard_map/all_gather | solution.py:72
  154.5 2.3 %copy.22 = bf16[4,1,512,256]{2,3,0,1:T(8,128)(2,1)} copy(bf16[4,1,512,256]{3,2,1,0:T(8,128)(2,1)} %all-gather.6.cloned.1.call-done) | data formatting | bytes 2097152 | tf_op jit(solution)/shard_map/all_gather | solution.py:72
  156.8 22.4 %all-gather.8.cloned.1.call-done = bf16[1024,512]{1,0:T(8,128)(2,1)} async-done(((bf16[128,512]{1,0:T(8,128)(2,1)}), bf16[1024,512]{1,0:T(8,128)(2,1)}) %all-gather.8.cloned.1.call-update) | async-done | bytes 1048592 | tf_op jit(solution)/shard_map/all_gather | solution.py:73
  179.2 3.1 %fusion.24 = bf16[1,512,512]{2,1,0:T(8,128)(2,1)} fusion(bf16[512,1024]{0,1:T(8,128)(2,1)} %bitcast.47, bf16[1024,512]{1,0:T(8,128)(2,1)} %all-gather.8.cloned.1.call-done), kind=kOutput, calls=%fused_computation.31 | convolution fusion | flops 537133056 | bytes 2621440 | tf_op jit(solution)/shard_map/blr,rc->blc/dot_general | solution.py:74
  (16 shorter events, 0.1 us)
Async XLA Ops:
  6.5 53.7 %copy-start = (bf16[2048,3,256]{2,0,1:T(8,128)(2,1)S(1)}, bf16[2048,3,256]{2,0,1:T(8,128)(2,1)}, u32[]{:S(2)}) copy-start(bf16[2048,3,256]{2,0,1:T(8,128)(2,1)} %param.5) | copy-start | bytes 9437188
  6.5 50.8 %all-gather.4.cloned.1.call-start = ((), (), s32[]{:S(2)}) async-start(), calls=%async_computation | async-start | bytes 2621440 | tf_op jit(solution)/shard_map/all_gather | solution.py:59
  7.3 147.3 %all-gather.6.cloned.1.call-start = ((), (), s32[]{:S(2)}) async-start(), calls=%async_computation.1 | async-start | bytes 1310720 | tf_op jit(solution)/shard_map/all_gather | solution.py:72
  57.3 2.2 %copy-start.1 = (bf16[1,512,2048]{2,1,0:T(8,128)(2,1)S(1)}, bf16[1,512,2048]{2,1,0:T(8,128)(2,1)}, u32[]{:S(2)}) copy-start(bf16[1,512,2048]{2,1,0:T(8,128)(2,1)} %all-gather.4.cloned.1.call-done) | copy-start | bytes 6291460
  60.2 15.2 %copy-start.4 = (bf16[3,2,256]{2,1,0:T(2,128)(2,1)S(1)}, bf16[3,2,256]{2,1,0:T(2,128)(2,1)}, u32[]{:S(2)}) copy-start(bf16[3,2,256]{2,1,0:T(2,128)(2,1)} %param.6) | copy-start | bytes 9220
  62.2 4.1 %copy-start.3 = (bf16[1,3,512,256]{2,3,1,0:T(8,128)(2,1)}, bf16[1,3,512,256]{2,3,1,0:T(8,128)(2,1)S(1)}, u32[]{:S(2)}) copy-start(bf16[1,3,512,256]{2,3,1,0:T(8,128)(2,1)S(1)} %fusion.21) | copy-start | bytes 2359300
  62.3 0.9 copy-start.2
  63.2 3.2 %collective-permute-start = (bf16[1,2,512,256]{2,3,1,0:T(8,128)(2,1)S(1)}, bf16[1,2,512,256]{2,3,1,0:T(8,128)(2,1)}, u32[]{:S(2)}, u32[]{:S(2)}) collective-permute-start(bf16[1,2,512,256]{2,3,1,0:T(8,128)(2,1)S(1)} %slice.16), channel_id=1, source_target_pairs={{0,4},{4,8},{8,12},{12,16},{16,20},{20,24},{24,28},{1,5},{5,9},{9,... | collective-permute-start | bytes 1572872 | tf_op jit(solution)/shard_map/ppermute | solution.py:13
  66.4 10.1 %collective-permute-start.1 = (bf16[1,2,512,256]{2,3,1,0:T(8,128)(2,1)}, bf16[1,2,512,256]{2,3,1,0:T(8,128)(2,1)}, u32[]{:S(2)}, u32[]{:S(2)}) collective-permute-start(bf16[1,2,512,256]{2,3,1,0:T(8,128)(2,1)} %collective-permute-done), channel_id=1, source_target_pairs={{0,4},{4,8},{8,12},{12,16},{16,20},{20,24},{24,28},{1,5},{5,9},{9,... | collective-permute-start | bytes 1572872 | tf_op jit(solution)/shard_map/ppermute | solution.py:13
  91.1 23.1 %collective-permute-start.2 = (bf16[1,2,512,256]{2,3,1,0:T(8,128)(2,1)}, bf16[1,2,512,256]{2,3,1,0:T(8,128)(2,1)S(1)}, u32[]{:S(2)}, u32[]{:S(2)}) collective-permute-start(bf16[1,2,512,256]{2,3,1,0:T(8,128)(2,1)} %bitcast.51), channel_id=1, source_target_pairs={{0,8},{4,12},{8,16},{12,20},{16,24},{20,28},{1,9},{5,13},{9,17},{1... | collective-permute-start | bytes 1572872 | tf_op jit(solution)/shard_map/ppermute | solution.py:13
  127.6 51.6 %all-gather.8.cloned.1.call-start = ((), (), s32[]{:S(2)}) async-start(), calls=%async_computation.2 | async-start | bytes 1179648 | tf_op jit(solution)/shard_map/all_gather | solution.py:73
Sparse Core Ops, SparseCore 0:
  8.9 48.3 all-gather.3
  127.7 26.7 all-gather.5
  156.4 22.7 all-gather.7
